TPU v7x, 32 devices: a whole 2x2x4 slice. The times are simulated.
32 devices in a mesh: snap: 2 (over y), row: 4 (over z), col: 4 (over x, core).
Axes of the slice: x: 2, y: 2, z: 4, core: 2. Of those that a mesh axis runs over, the one named last changes fastest.
Arguments:
- orbitals: float32 [12288, 768], P(('snap', 'row', 'col')), parts along dimension 0, may hold values from -6 to 6
- screened: float32 [6, 6144, 6144], P('snap', 'row', 'col'), parts along dimension 0, may hold values from -0.0029296875 to 0.0029296875
- green_weight: float32 [6, 768], P('snap'), parts along dimension 0, may hold values from 0.05 to 1
- time_weight: float32 [3], replicated, may hold values from 0.3 to 1
Outputs:
- updated: float32 [12288, 768], P(('snap', 'row', 'col')), parts along dimension 0
There are 2 independent parts, one for each index of `snap`. A program takes and returns all parts, laid end to end along the dimension named above; an argument that names none is the same for every part. Nothing has to cross between parts.
All inputs are finite; a program needn't handle non-finite values.
Results may differ from a plain program's by a relative error of at most 0.00013.
Values sent between devices are 32-bit elements; how exact they have to be, the bound alone decides.
A program may use at most 128 MiB of HBM per device.

v0:
```python
import jax
import jax.numpy as jnp
from jax import lax
from jax.sharding import PartitionSpec as P

TIMES = 3
PASSES = 2


def from_root(block, axis, owner):
    block = jnp.where(lax.axis_index(axis) == owner, block, jnp.zeros_like(block))
    return lax.psum(block, axis)


def gather_rows(shard):
    return lax.all_gather(shard, "col", axis=0, tiled=True)


def scatter_rows(partial_value):
    return lax.psum_scatter(partial_value, "col", scatter_dimension=0, tiled=True)


def body(orbitals, screened, green_weight, time_weight):
    n_row = lax.axis_size("row")
    n_col = lax.axis_size("col")
    factor = n_col // n_row
    col_width = screened.shape[2]
    col_index = lax.axis_index("col")
    root = col_index // factor
    offset = col_index % factor * col_width
    own = orbitals
    rows = gather_rows(own)
    for step in range(PASSES):
        piece = lax.dynamic_slice_in_dim(rows, offset, col_width, 0)
        columns = from_root(piece, "row", root)
        partial_value = jnp.zeros(rows.shape, jnp.float32)
        for t in range(TIMES):
            green = lax.dot_general(
                rows * green_weight[t],
                columns,
                (((1,), (1,)), ((), ())),
                precision=lax.Precision.HIGHEST,
                preferred_element_type=jnp.float32,
            )
            applied = jnp.dot(
                green * screened[t],
                columns,
                precision=lax.Precision.HIGHEST,
                preferred_element_type=jnp.float32,
            )
            partial_value = partial_value + time_weight[t] * applied
        final = step == PASSES - 1
        own = own - scatter_rows(partial_value)
        if not final:
            rows = gather_rows(own)
    return own


def solution(mesh):
    in_specs = (P(("snap", "row", "col"), None), P("snap", "row", "col"), P("snap", None), P())
    out_specs = P(("snap", "row", "col"), None)
    return jax.shard_map(body, mesh=mesh, in_specs=in_specs, out_specs=out_specs, check_vma=False)
```

profile of v0, /device:TPU:0, one launch (start us, length us, event | category | flops | bytes accessed | tf_op | source)
XLA Modules:
  0.0 877.8 jit_solution(2341078948588468849)
XLA Ops:
  6.5 0.0 all-gather.3.cloned.1.call-start
  6.5 0.7 all-gather.3.cloned.1.call-update
  7.3 0.0 all-reduce.3.cloned.1.call-start
  7.3 41.8 %all-gather.3.cloned.1.call-done = f32[1536,768]{1,0:T(8,128)} async-done(((f32[384,768]{1,0:T(8,128)}), f32[1536,768]{1,0:T(8,128)}) %all-gather.3.cloned.1.call-update) | async-done | bytes 4718608 | tf_op jit(solution)/shard_map/all_gather | solution.py:16
  49.1 4.8 broadcast_select_fusion.1
  53.9 0.0 all-reduce.3.cloned.1.call-update
  53.9 0.0 reduce-scatter.3.cloned.1.call-start
  53.9 0.6 copy-done.4
  54.5 0.6 fusion.12
  55.2 0.0 copy-done.3
  55.2 170.7 %all-reduce.3.cloned.1.call-done = f32[1536,768]{1,0:T(8,128)} async-done(((f32[1536,768]{1,0:T(8,128)}), f32[1536,768]{1,0:T(8,128)}) %all-reduce.3.cloned.1.call-update) | async-done | bytes 4718608 | tf_op jit(solution)/shard_map/psum | solution.py:12
  225.9 28.3 %convolution_multiply_fusion.4 = f32[1536,1536]{1,0:T(8,128)} fusion(f32[1536,768]{1,0:T(8,128)} %all-reduce.3.cloned.1.call-done, f32[3,1536,1536]{2,1,0:T(8,128)} %param.5, f32[1536,768]{1,0:T(8,128)} %all-gather.3.cloned.1.call-done, f32[768]{0:T(1024)S(1)} %get-tuple-element.7), kind=kOutput, calls=%fused_computation.4 | convolution fusion | flops 21746810880 | bytes 28314624 | tf_op jit(solution)/shard_map/dot_general | solution.py:38
  254.2 28.0 %fusion.14 = f32[1536,768]{1,0:T(8,128)} fusion(f32[1536,1536]{1,0:T(8,128)} %convolution_multiply_fusion.4, f32[1536,768]{1,0:T(8,128)} %all-reduce.3.cloned.1.call-done), kind=kOutput, calls=%fused_computation.27 | convolution fusion | flops 21743271936 | bytes 18874368 | tf_op jit(solution)/shard_map/dot_general | solution.py:45
  282.2 0.0 slice-done.7
  282.2 0.0 slice-done
  282.2 0.0 slice-done.1
  282.2 0.0 slice-done.2
  282.2 0.0 slice-done.3
  282.2 0.0 slice-done.8
  282.2 0.0 slice-done.4
  282.2 26.8 %convolution_multiply_fusion.5 = f32[1536,1536]{1,0:T(8,128)} fusion(f32[1536,768]{1,0:T(8,128)} %all-reduce.3.cloned.1.call-done, f32[3,1536,1536]{2,1,0:T(8,128)S(1)} %bitcast.31, f32[1536,768]{1,0:T(8,128)S(1)} %bitcast.33, f32[768]{0:T(1024)S(1)} %get-tuple-element.6), kind=kOutput, calls=%fused_computation.5 | convolution fusion | flops 21746810880 | bytes 28314624 | tf_op jit(solution)/shard_map/dot_general | solution.py:38
  309.0 27.7 %fusion.13 = f32[1536,768]{1,0:T(8,128)} fusion(f32[1536,1536]{1,0:T(8,128)} %convolution_multiply_fusion.5, f32[1536,768]{1,0:T(8,128)} %all-reduce.3.cloned.1.call-done), kind=kOutput, calls=%fused_computation.26 | convolution fusion | flops 21743271936 | bytes 18874368 | tf_op jit(solution)/shard_map/dot_general | solution.py:45
  336.8 27.0 %convolution_multiply_fusion.3 = f32[1536,1536]{1,0:T(8,128)} fusion(f32[1536,768]{1,0:T(8,128)} %all-reduce.3.cloned.1.call-done, f32[3,1536,1536]{2,1,0:T(8,128)S(1)} %bitcast.31, f32[1536,768]{1,0:T(8,128)S(1)} %bitcast.33, f32[768]{0:T(1024)S(1)} %get-tuple-element.5), kind=kOutput, calls=%fused_computation.3 | convolution fusion | flops 21746810880 | bytes 28314624 | tf_op jit(solution)/shard_map/dot_general | solution.py:38
  363.8 31.6 %multiply_add_fusion.1 = f32[1536,768]{1,0:T(8,128)} fusion(f32[1536,768]{1,0:T(8,128)} %fusion.14, f32[1536,768]{1,0:T(8,128)} %fusion.13, f32[1536,1536]{1,0:T(8,128)} %convolution_multiply_fusion.3, f32[1536,768]{1,0:T(8,128)} %all-reduce.3.cloned.1.call-done, f32[]{:T(128)} %bitcast.4, f32[]{:T(128)} %bitcast.2, f32[]{:T(128)} %bitcast), kind=kOutput, calls=%fused_computation.10 | convolution fusion | flops 21749170176 | bytes 28311564 | tf_op jit(solution)/shard_map/dot_general | solution.py:45
  395.4 0.0 copy-start.2
  395.4 0.0 reduce-scatter.3.cloned.1.call-update
  395.4 0.0 all-gather.5.cloned.1.call-start
  395.5 47.0 %reduce-scatter.3.cloned.1.call-done = f32[384,768]{1,0:T(8,128)} async-done(((f32[1536,768]{1,0:T(8,128)}), f32[384,768]{1,0:T(8,128)}) %reduce-scatter.3.cloned.1.call-update) | async-done | bytes 1179664 | tf_op jit(solution)/shard_map/reduce_scatter | solution.py:20
  442.5 2.4 sub.8
  444.9 0.0 all-gather.5.cloned.1.call-update
  445.0 0.0 all-reduce.5.cloned.1.call-start
  445.0 37.5 %all-gather.5.cloned.1.call-done = f32[1536,768]{1,0:T(8,128)} async-done(((f32[384,768]{1,0:T(8,128)}), f32[1536,768]{1,0:T(8,128)}) %all-gather.5.cloned.1.call-update) | async-done | bytes 4718608 | tf_op jit(solution)/shard_map/all_gather | solution.py:16
  482.5 4.8 broadcast_select_fusion
  487.4 0.0 all-reduce.5.cloned.1.call-update
  487.4 0.0 reduce-scatter.5.cloned.1.call-start
  487.5 171.9 %all-reduce.5.cloned.1.call-done = f32[1536,768]{1,0:T(8,128)} async-done(((f32[1536,768]{1,0:T(8,128)}), f32[1536,768]{1,0:T(8,128)}) %all-reduce.5.cloned.1.call-update) | async-done | bytes 4718608 | tf_op jit(solution)/shard_map/psum | solution.py:12
  659.4 27.4 %convolution_multiply_fusion.1 = f32[1536,1536]{1,0:T(8,128)S(1)} fusion(f32[1536,768]{1,0:T(8,128)} %all-reduce.5.cloned.1.call-done, f32[3,1536,1536]{2,1,0:T(8,128)} %param.5, f32[1536,768]{1,0:T(8,128)} %all-gather.5.cloned.1.call-done, f32[768]{0:T(1024)S(1)} %get-tuple-element.7), kind=kOutput, calls=%fused_computation.1 | convolution fusion | flops 21746810880 | bytes 28314624 | tf_op jit(solution)/shard_map/dot_general | solution.py:38
  686.8 0.0 copy-done
  686.8 0.0 slice-start.10
  686.8 27.3 %convolution_multiply_fusion.2 = f32[1536,1536]{1,0:T(8,128)} fusion(f32[1536,768]{1,0:T(8,128)S(1)} %copy-done, f32[3,1536,1536]{2,1,0:T(8,128)} %param.5, f32[1536,768]{1,0:T(8,128)} %all-gather.5.cloned.1.call-done, f32[768]{0:T(1024)S(1)} %get-tuple-element.6), kind=kOutput, calls=%fused_computation.2 | convolution fusion | flops 21746810880 | bytes 28314624 | tf_op jit(solution)/shard_map/dot_general | solution.py:38
  714.1 0.0 slice-done.10
  714.2 28.4 %convolution_multiply_fusion = f32[1536,1536]{1,0:T(8,128)S(1)} fusion(f32[1536,768]{1,0:T(8,128)S(1)} %copy-done, f32[3,1536,1536]{2,1,0:T(8,128)} %param.5, f32[1536,768]{1,0:T(8,128)S(1)} %bitcast.35, f32[768]{0:T(1024)S(1)} %get-tuple-element.5), kind=kOutput, calls=%fused_computation | convolution fusion | flops 21746810880 | bytes 28314624 | tf_op jit(solution)/shard_map/dot_general | solution.py:38
  742.6 23.3 %fusion.16 = f32[1536,768]{1,0:T(8,128)S(1)} fusion(f32[1536,1536]{1,0:T(8,128)S(1)} %convolution_multiply_fusion.1, f32[1536,768]{1,0:T(8,128)S(1)} %copy-done), kind=kOutput, calls=%fused_computation.29 | convolution fusion | flops 21743271936 | bytes 18874368 | tf_op jit(solution)/shard_map/dot_general | solution.py:45
  765.9 28.4 %fusion.15 = f32[1536,768]{1,0:T(8,128)S(1)} fusion(f32[1536,1536]{1,0:T(8,128)} %convolution_multiply_fusion.2, f32[1536,768]{1,0:T(8,128)S(1)} %copy-done), kind=kOutput, calls=%fused_computation.28 | convolution fusion | flops 21743271936 | bytes 18874368 | tf_op jit(solution)/shard_map/dot_general | solution.py:45
  794.2 27.0 %multiply_add_fusion = f32[1536,768]{1,0:T(8,128)} fusion(f32[1536,768]{1,0:T(8,128)S(1)} %fusion.16, f32[1536,768]{1,0:T(8,128)S(1)} %fusion.15, f32[1536,1536]{1,0:T(8,128)S(1)} %convolution_multiply_fusion, f32[1536,768]{1,0:T(8,128)S(1)} %copy-done, f32[]{:T(128)} %bitcast.4, f32[]{:T(128)} %bitcast.2, f32[]{:T(128)} %bitcast), kind=kOutput, calls=%fused_computation.6 | convolution fusion | flops 21749170176 | bytes 28311564 | tf_op jit(solution)/shard_map/dot_general | solution.py:45
  821.2 0.0 reduce-scatter.5.cloned.1.call-update
  821.2 47.1 %reduce-scatter.5.cloned.1.call-done = f32[384,768]{1,0:T(8,128)} async-done(((f32[1536,768]{1,0:T(8,128)}), f32[384,768]{1,0:T(8,128)}) %reduce-scatter.5.cloned.1.call-update) | async-done | bytes 1179664 | tf_op jit(solution)/shard_map/reduce_scatter | solution.py:20
  868.3 2.4 sub.9
  (23 shorter events, 0.1 us)
Async XLA Ops:
  6.5 42.5 %all-gather.3.cloned.1.call-start = ((), (), s32[]{:S(2)}) async-start(), calls=%async_computation.2 | async-start | bytes 5898240 | tf_op jit(solution)/shard_map/all_gather | solution.py:16
  7.3 218.6 %all-reduce.3.cloned.1.call-start = ((), (), s32[]{:S(2)}) async-start(), calls=%async_computation.3 | async-start | bytes 9437184 | tf_op jit(solution)/shard_map/psum | solution.py:12
  53.9 0.7 copy-start.4
  53.9 1.3 copy-start.3
  53.9 228.3 %slice-start.7 = ((s8[4718592]{0:T(1024)(128)(4,1)}), s8[524288]{0:T(1024)(128)(4,1)S(1)}, s32[]{:S(2)}) async-start(s8[4718592]{0:T(1024)(128)(4,1)} %bitcast.32), calls=%async_computation.15 | async-start | bytes 1048576
  53.9 388.6 %reduce-scatter.3.cloned.1.call-start = ((), (), s32[]{:S(2)}) async-start(), calls=%async_computation.4 | async-start | bytes 5898240 | tf_op jit(solution)/shard_map/reduce_scatter | solution.py:20
  225.9 56.3 %slice-start = ((s8[28311552]{0:T(1024)(128)(4,1)}), s8[4194304]{0:T(1024)(128)(4,1)S(1)}, s32[]{:S(2)}) async-start(s8[28311552]{0:T(1024)(128)(4,1)} %bitcast.30), calls=%async_computation.8 | async-start | bytes 8388608
  225.9 56.3 %slice-start.1 = ((s8[28311552]{0:T(1024)(128)(4,1)}), s8[4194304]{0:T(1024)(128)(4,1)S(1)}, s32[]{:S(2)}) async-start(s8[28311552]{0:T(1024)(128)(4,1)} %bitcast.30), calls=%async_computation.9 | async-start | bytes 8388608
  225.9 56.3 %slice-start.2 = ((s8[28311552]{0:T(1024)(128)(4,1)}), s8[4194304]{0:T(1024)(128)(4,1)S(1)}, s32[]{:S(2)}) async-start(s8[28311552]{0:T(1024)(128)(4,1)} %bitcast.30), calls=%async_computation.10 | async-start | bytes 8388608
  225.9 56.3 %slice-start.3 = ((s8[28311552]{0:T(1024)(128)(4,1)}), s8[4194304]{0:T(1024)(128)(4,1)S(1)}, s32[]{:S(2)}) async-start(s8[28311552]{0:T(1024)(128)(4,1)} %bitcast.30), calls=%async_computation.11 | async-start | bytes 8388608
  225.9 56.3 %slice-start.8 = ((s8[4718592]{0:T(1024)(128)(4,1)}), s8[4194304]{0:T(1024)(128)(4,1)S(1)}, s32[]{:S(2)}) async-start(s8[4718592]{0:T(1024)(128)(4,1)} %bitcast.32), calls=%async_computation.16 | async-start | bytes 8388608
  254.1 28.0 %slice-start.4 = ((s8[28311552]{0:T(1024)(128)(4,1)}), s8[4194304]{0:T(1024)(128)(4,1)S(1)}, s32[]{:S(2)}) async-start(s8[28311552]{0:T(1024)(128)(4,1)} %bitcast.30), calls=%async_computation.12 | async-start | bytes 8388608
  254.1 28.1 %slice-start.5 = ((s8[28311552]{0:T(1024)(128)(4,1)}), s8[4194304]{0:T(1024)(128)(4,1)S(1)}, s32[]{:S(2)}) async-start(s8[28311552]{0:T(1024)(128)(4,1)} %bitcast.30), calls=%async_computation.13 | async-start | bytes 8388608
  254.2 28.1 %slice-start.6 = ((s8[28311552]{0:T(1024)(128)(4,1)}), s8[3145728]{0:T(1024)(128)(4,1)S(1)}, s32[]{:S(2)}) async-start(s8[28311552]{0:T(1024)(128)(4,1)} %bitcast.30), calls=%async_computation.14 | async-start | bytes 6291456
  395.4 47.1 %copy-start.2 = (f32[384,768]{1,0:T(8,128)S(1)}, f32[384,768]{1,0:T(8,128)}, u32[]{:S(2)}) copy-start(f32[384,768]{1,0:T(8,128)} %param.4) | copy-start | bytes 3538948
  395.4 87.1 %all-gather.5.cloned.1.call-start = ((), (), s32[]{:S(2)}) async-start(), calls=%async_computation.5 | async-start | bytes 5898240 | tf_op jit(solution)/shard_map/all_gather | solution.py:16
  445.0 214.4 %all-reduce.5.cloned.1.call-start = ((), (), s32[]{:S(2)}) async-start(), calls=%async_computation.6 | async-start | bytes 9437184 | tf_op jit(solution)/shard_map/psum | solution.py:12
  487.4 380.9 %reduce-scatter.5.cloned.1.call-start = ((), (), s32[]{:S(2)}) async-start(), calls=%async_computation.7 | async-start | bytes 5898240 | tf_op jit(solution)/shard_map/reduce_scatter | solution.py:20
  659.4 27.4 %copy-start = (f32[1536,768]{1,0:T(8,128)S(1)}, f32[1536,768]{1,0:T(8,128)}, u32[]{:S(2)}) copy-start(f32[1536,768]{1,0:T(8,128)} %all-reduce.5.cloned.1.call-done) | copy-start | bytes 14155780
  659.4 54.8 %slice-start.9 = ((s8[4718592]{0:T(1024)(128)(4,1)}), s8[4194304]{0:T(1024)(128)(4,1)S(1)}, s32[]{:S(2)}) async-start(s8[4718592]{0:T(1024)(128)(4,1)} %bitcast.34), calls=%async_computation.17 | async-start | bytes 8388608
  686.8 27.3 %slice-start.10 = ((s8[4718592]{0:T(1024)(128)(4,1)}), s8[524288]{0:T(1024)(128)(4,1)S(1)}, s32[]{:S(2)}) async-start(s8[4718592]{0:T(1024)(128)(4,1)} %bitcast.34), calls=%async_computation.18 | async-start | bytes 1048576
  821.2 47.1 %copy-start.1 = (f32[384,768]{1,0:T(8,128)S(1)}, f32[384,768]{1,0:T(8,128)}, u32[]{:S(2)}) copy-start(f32[384,768]{1,0:T(8,128)} %sub.8) | copy-start | bytes 3538948
Sparse Core Ops, SparseCore 0:
  8.9 40.1 all-gather.2
  54.0 171.8 all-reduce.2
  395.5 46.9 reduce-scatter.2
  445.1 37.4 all-gather.4
  487.5 171.8 all-reduce.4
  821.4 46.9 reduce-scatter.4
where the time goes:
time: 886 us; the launch traced here: 878 us
  waiting for transfers between devices  517 us (58%)
  matrix products  331 us (37%)
  other arithmetic  14.5 us (2%)
  between operations  13.9 us (2%)
    psum x2, waiting for transfers between devices, from_root(): return lax.psum(block, axis)  343 us
    dot_general x6, matrix products, body(): jnp.dot(green * screened[t], columns, precision=lax.Precision.HIGHEST, pr...  166 us
    dot_general x6, matrix products, body(): lax.dot_general(rows * green_weight[t], columns, (((1,), (1,)), ((), ()))...  165 us
    reduce_scatter x2, waiting for transfers between devices, scatter_rows(): lax.psum_scatter(partial_value, 'col', scatter_dimension=0, tiled=True)  94.1 us
    all_gather x2, waiting for transfers between devices, gather_rows(): return lax.all_gather(shard, 'col', axis=0, tiled=True)  79.3 us
  transfers between devices with their start and end apart: 6, of which 6 were waited for; matrix products, arithmetic and copies ran while one was open for 0% of the time, Pallas kernels for 0%

commit v1 on v0

--- a/solution.py
+++ b/solution.py
@@ -7,13 +7,30 @@
 PASSES = 2
 
 
+def joined_along(pieces, dim):
+    lengths = list(pieces.shape[1:])
+    lengths[dim] *= pieces.shape[0]
+    return jnp.moveaxis(pieces, 0, dim).reshape(lengths)
+
+
+def ring_gather(x, axis, dim):
+    size = lax.axis_size(axis)
+    ahead = [(i, (i + 1) % size) for i in range(size)]
+    pieces = [x]
+    while len(pieces) < size:
+        pieces.append(lax.ppermute(pieces[-1], axis, ahead))
+    index = lax.axis_index(axis)
+    pieces = jnp.stack(pieces)[(index - jnp.arange(size)) % size]
+    return joined_along(pieces, dim)
+
+
 def from_root(block, axis, owner):
     block = jnp.where(lax.axis_index(axis) == owner, block, jnp.zeros_like(block))
     return lax.psum(block, axis)
 
 
 def gather_rows(shard):
-    return lax.all_gather(shard, "col", axis=0, tiled=True)
+    return ring_gather(shard, "col", 0)
 
 
 def scatter_rows(partial_value):

time: 886 us -> 928 us (1.047)
  waiting for transfers between devices: 517 us -> 532 us
  other arithmetic: 14.5 us -> 28.1 us
  local copies, waits for them, and re-layouts: 1.3 us -> 12.9 us
    ppermute x0 -> x6, waiting for transfers between devices: none -> 93.2 us  [ring_gather(): pieces.append(lax.ppermute(pieces[-1], axis, ahead))]
    all_gather x2 -> x0, waiting for transfers between devices: 79.3 us -> none  [gather_rows(): return lax.all_gather(shard, 'col', axis=0, tiled=True)]
    mul x0 -> x2, other arithmetic: none -> 18 us  [body(): rows * green_weight[t]]
    gather x0 -> x2, local copies, waits for them, and re-layouts: none -> 10.7 us  [ring_gather(): pieces = jnp.stack(pieces)[(index - jnp.arange(size)) % size]]
    select_n x2 -> x1, other arithmetic: 9.63 us -> 0.01 us  [ring_gather(): pieces = jnp.stack(pieces)[(index - jnp.arange(size)) % size]]
  transfers between devices with their start and end apart: 6 -> 10, of which waited for: 6 -> 10; matrix products, arithmetic and copies ran while one was open for 0% -> 0% of each run, Pallas kernels for 0% -> 0%
where the time goes in v1:
time: 928 us; the launch traced here: 921 us
  waiting for transfers between devices  532 us (57%)
  matrix products  333 us (36%)
  other arithmetic  28.1 us (3%)
  between operations  13.8 us (1%)
  local copies, waits for them, and re-layouts  12.9 us (1%)
    psum x2, waiting for transfers between devices, from_root(): return lax.psum(block, axis)  345 us
    dot_general x6, matrix products, body(): jnp.dot(green * screened[t], columns, precision=lax.Precision.HIGHEST, pr...  168 us
    dot_general x6, matrix products, body(): lax.dot_general(rows * green_weight[t], columns, (((1,), (1,)), ((), ()))...  165 us
    reduce_scatter x2, waiting for transfers between devices, scatter_rows(): lax.psum_scatter(partial_value, 'col', scatter_dimension=0, tiled=True)  94.1 us
    ppermute x6, waiting for transfers between devices, ring_gather(): pieces.append(lax.ppermute(pieces[-1], axis, ahead))  93.2 us
  transfers between devices with their start and end apart: 10, of which 10 were waited for; matrix products, arithmetic and copies ran while one was open for 0% of the time, Pallas kernels for 0%

profile of v1, /device:TPU:0, one launch (start us, length us, event | category | flops | bytes accessed | tf_op | source)
XLA Modules:
  0.0 921.1 jit_solution(10202379554436037249)
XLA Ops:
  6.5 0.5 collective-permute-start
  7.0 16.0 %collective-permute-done = f32[384,768]{1,0:T(8,128)S(1)} collective-permute-done((f32[384,768]{1,0:T(8,128)}, f32[384,768]{1,0:T(8,128)S(1)}, u32[]{:S(2)}, u32[]{:S(2)}) %collective-permute-start) | collective-permute-done | bytes 1179680 | tf_op jit(solution)/shard_map/ppermute | solution.py:21
  23.0 0.0 collective-permute-start.1
  23.1 15.6 %collective-permute-done.1 = f32[384,768]{1,0:T(8,128)S(1)} collective-permute-done((f32[384,768]{1,0:T(8,128)S(1)}, f32[384,768]{1,0:T(8,128)S(1)}, u32[]{:S(2)}, u32[]{:S(2)}) %collective-permute-start.1) | collective-permute-done | bytes 1179680 | tf_op jit(solution)/shard_map/ppermute | solution.py:21
  38.7 0.0 collective-permute-start.2
  38.7 0.8 slice_reduce_fusion
  39.6 14.7 %collective-permute-done.2 = f32[384,768]{1,0:T(8,128)S(1)} collective-permute-done((f32[384,768]{1,0:T(8,128)S(1)}, f32[384,768]{1,0:T(8,128)S(1)}, u32[]{:S(2)}, u32[]{:S(2)}) %collective-permute-start.2) | collective-permute-done | bytes 1179680 | tf_op jit(solution)/shard_map/ppermute | solution.py:21
  54.3 3.7 pad_maximum_fusion
  58.0 5.4 gather_fusion
  63.4 9.0 bitcast_multiply_fusion.3
  72.4 0.0 all-reduce.3.cloned.1.call-update
  72.4 0.0 reduce-scatter.3.cloned.1.call-start
  72.5 0.6 copy-done.5
  73.0 0.7 fusion.2
  73.7 172.9 %all-reduce.3.cloned.1.call-done = f32[1536,768]{1,0:T(8,128)} async-done(((f32[1536,768]{1,0:T(8,128)}), f32[1536,768]{1,0:T(8,128)}) %all-reduce.3.cloned.1.call-update) | async-done | bytes 4718608 | tf_op jit(solution)/shard_map/psum | solution.py:29
  246.6 28.3 %convolution_multiply_fusion.4 = f32[1536,1536]{1,0:T(8,128)} fusion(f32[1536,768]{1,0:T(8,128)} %get-tuple-element.14, f32[1536,768]{1,0:T(8,128)} %all-reduce.3.cloned.1.call-done, f32[3,1536,1536]{2,1,0:T(8,128)} %param.5), kind=kOutput, calls=%fused_computation.6 | convolution fusion | flops 21745631232 | bytes 28311552 | tf_op jit(solution)/shard_map/dot_general | solution.py:55
  274.9 0.0 slice-start.6
  274.9 27.0 %fusion.4 = f32[1536,768]{1,0:T(8,128)} fusion(f32[1536,1536]{1,0:T(8,128)} %convolution_multiply_fusion.4, f32[1536,768]{1,0:T(8,128)S(1)} %copy-done), kind=kOutput, calls=%fused_computation.32 | convolution fusion | flops 21743271936 | bytes 18874368 | tf_op jit(solution)/shard_map/dot_general | solution.py:62
  302.0 27.2 %convolution_multiply_fusion.5 = f32[1536,1536]{1,0:T(8,128)} fusion(f32[1536,768]{1,0:T(8,128)} %get-tuple-element.15, f32[1536,768]{1,0:T(8,128)S(1)} %copy-done, f32[3,1536,1536]{2,1,0:T(8,128)S(1)} %bitcast.57), kind=kOutput, calls=%fused_computation.7 | convolution fusion | flops 21745631232 | bytes 28311552 | tf_op jit(solution)/shard_map/dot_general | solution.py:55
  329.1 27.1 %fusion.3 = f32[1536,768]{1,0:T(8,128)} fusion(f32[1536,1536]{1,0:T(8,128)} %convolution_multiply_fusion.5, f32[1536,768]{1,0:T(8,128)S(1)} %copy-done), kind=kOutput, calls=%fused_computation.31 | convolution fusion | flops 21743271936 | bytes 18874368 | tf_op jit(solution)/shard_map/dot_general | solution.py:62
  356.2 27.1 %convolution_multiply_fusion.3 = f32[1536,1536]{1,0:T(8,128)} fusion(f32[1536,768]{1,0:T(8,128)} %get-tuple-element.12, f32[1536,768]{1,0:T(8,128)S(1)} %copy-done, f32[3,1536,1536]{2,1,0:T(8,128)S(1)} %bitcast.57), kind=kOutput, calls=%fused_computation.5 | convolution fusion | flops 21745631232 | bytes 28311552 | tf_op jit(solution)/shard_map/dot_general | solution.py:55
  383.3 29.9 %multiply_add_fusion.1 = f32[1536,768]{1,0:T(8,128)} fusion(f32[1536,768]{1,0:T(8,128)} %fusion.4, f32[1536,768]{1,0:T(8,128)} %fusion.3, f32[1536,1536]{1,0:T(8,128)} %convolution_multiply_fusion.3, f32[1536,768]{1,0:T(8,128)S(1)} %copy-done, f32[]{:T(128)} %bitcast.10, f32[]{:T(128)} %bitcast.8, f32[]{:T(128)} %bitcast), kind=kOutput, calls=%fused_computation.19 | convolution fusion | flops 21749170176 | bytes 28311564 | tf_op jit(solution)/shard_map/dot_general | solution.py:62
  413.2 0.0 reduce-scatter.3.cloned.1.call-update
  413.2 0.0 all-reduce.5.cloned.1.call-start
  413.2 47.0 %reduce-scatter.3.cloned.1.call-done = f32[384,768]{1,0:T(8,128)} async-done(((f32[1536,768]{1,0:T(8,128)}), f32[384,768]{1,0:T(8,128)}) %reduce-scatter.3.cloned.1.call-update) | async-done | bytes 1179664 | tf_op jit(solution)/shard_map/reduce_scatter | solution.py:37
  460.3 1.4 sub.25
  461.7 0.0 copy-start.2
  461.7 0.1 collective-permute-start.3
  461.7 15.6 %collective-permute-done.3 = f32[384,768]{1,0:T(8,128)S(1)} collective-permute-done((f32[384,768]{1,0:T(8,128)S(1)}, f32[384,768]{1,0:T(8,128)S(1)}, u32[]{:S(2)}, u32[]{:S(2)}) %collective-permute-start.3) | collective-permute-done | bytes 1179680 | tf_op jit(solution)/shard_map/ppermute | solution.py:21
  477.4 0.0 collective-permute-start.4
  477.4 15.6 %collective-permute-done.4 = f32[384,768]{1,0:T(8,128)S(1)} collective-permute-done((f32[384,768]{1,0:T(8,128)S(1)}, f32[384,768]{1,0:T(8,128)S(1)}, u32[]{:S(2)}, u32[]{:S(2)}) %collective-permute-start.4) | collective-permute-done | bytes 1179680 | tf_op jit(solution)/shard_map/ppermute | solution.py:21
  493.0 0.0 collective-permute-start.5
  493.0 15.6 %collective-permute-done.5 = f32[384,768]{1,0:T(8,128)S(1)} collective-permute-done((f32[384,768]{1,0:T(8,128)S(1)}, f32[384,768]{1,0:T(8,128)S(1)}, u32[]{:S(2)}, u32[]{:S(2)}) %collective-permute-start.5) | collective-permute-done | bytes 1179680 | tf_op jit(solution)/shard_map/ppermute | solution.py:21
  508.6 2.5 pad_maximum_fusion.1
  511.1 5.3 gather_fusion.1
  516.4 9.0 bitcast_multiply_fusion
  525.4 0.0 all-reduce.5.cloned.1.call-update
  525.5 0.0 reduce-scatter.5.cloned.1.call-start
  525.5 172.1 %all-reduce.5.cloned.1.call-done = f32[1536,768]{1,0:T(8,128)} async-done(((f32[1536,768]{1,0:T(8,128)}), f32[1536,768]{1,0:T(8,128)}) %all-reduce.5.cloned.1.call-update) | async-done | bytes 4718608 | tf_op jit(solution)/shard_map/psum | solution.py:29
  697.6 28.5 %convolution_multiply_fusion.1 = f32[1536,1536]{1,0:T(8,128)} fusion(f32[1536,768]{1,0:T(8,128)} %get-tuple-element.10, f32[1536,768]{1,0:T(8,128)} %all-reduce.5.cloned.1.call-done, f32[3,1536,1536]{2,1,0:T(8,128)} %param.5), kind=kOutput, calls=%fused_computation.3 | convolution fusion | flops 21745631232 | bytes 28311552 | tf_op jit(solution)/shard_map/dot_general | solution.py:55
  726.1 27.4 %fusion.6 = f32[1536,768]{1,0:T(8,128)} fusion(f32[1536,1536]{1,0:T(8,128)} %convolution_multiply_fusion.1, f32[1536,768]{1,0:T(8,128)S(1)} %copy-done.1), kind=kOutput, calls=%fused_computation.34 | convolution fusion | flops 21743271936 | bytes 18874368 | tf_op jit(solution)/shard_map/dot_general | solution.py:62
  753.6 27.1 %convolution_multiply_fusion.2 = f32[1536,1536]{1,0:T(8,128)} fusion(f32[1536,768]{1,0:T(8,128)} %get-tuple-element.11, f32[1536,768]{1,0:T(8,128)S(1)} %copy-done.1, f32[3,1536,1536]{2,1,0:T(8,128)S(1)} %bitcast.59), kind=kOutput, calls=%fused_computation.4 | convolution fusion | flops 21745631232 | bytes 28311552 | tf_op jit(solution)/shard_map/dot_general | solution.py:55
  780.6 26.8 %fusion.5 = f32[1536,768]{1,0:T(8,128)} fusion(f32[1536,1536]{1,0:T(8,128)} %convolution_multiply_fusion.2, f32[1536,768]{1,0:T(8,128)S(1)} %copy-done.1), kind=kOutput, calls=%fused_computation.33 | convolution fusion | flops 21743271936 | bytes 18874368 | tf_op jit(solution)/shard_map/dot_general | solution.py:62
  807.5 27.1 %convolution_multiply_fusion = f32[1536,1536]{1,0:T(8,128)} fusion(f32[1536,768]{1,0:T(8,128)} %get-tuple-element.8, f32[1536,768]{1,0:T(8,128)S(1)} %copy-done.1, f32[3,1536,1536]{2,1,0:T(8,128)S(1)} %bitcast.59), kind=kOutput, calls=%fused_computation.2 | convolution fusion | flops 21745631232 | bytes 28311552 | tf_op jit(solution)/shard_map/dot_general | solution.py:55
  834.6 30.0 %multiply_add_fusion = f32[1536,768]{1,0:T(8,128)} fusion(f32[1536,768]{1,0:T(8,128)} %fusion.6, f32[1536,768]{1,0:T(8,128)} %fusion.5, f32[1536,1536]{1,0:T(8,128)} %convolution_multiply_fusion, f32[1536,768]{1,0:T(8,128)S(1)} %copy-done.1, f32[]{:T(128)} %bitcast.10, f32[]{:T(128)} %bitcast.8, f32[]{:T(128)} %bitcast), kind=kOutput, calls=%fused_computation.18 | convolution fusion | flops 21749170176 | bytes 28311564 | tf_op jit(solution)/shard_map/dot_general | solution.py:62
  864.6 0.0 reduce-scatter.5.cloned.1.call-update
  864.6 47.1 %reduce-scatter.5.cloned.1.call-done = f32[384,768]{1,0:T(8,128)} async-done(((f32[1536,768]{1,0:T(8,128)}), f32[384,768]{1,0:T(8,128)}) %reduce-scatter.5.cloned.1.call-update) | async-done | bytes 1179664 | tf_op jit(solution)/shard_map/reduce_scatter | solution.py:37
  911.7 2.4 sub.26
  (42 shorter events, 0.1 us)
Async XLA Ops:
  6.5 240.0 %all-reduce.3.cloned.1.call-start = ((), (), s32[]{:S(2)}) async-start(), calls=%async_computation.2 | async-start | bytes 9437184 | tf_op jit(solution)/shard_map/psum | solution.py:29
  6.5 16.5 %collective-permute-start = (f32[384,768]{1,0:T(8,128)}, f32[384,768]{1,0:T(8,128)S(1)}, u32[]{:S(2)}, u32[]{:S(2)}) collective-permute-start(f32[384,768]{1,0:T(8,128)} %param.4), channel_id=1, source_target_pairs={{0,1},{1,2},{2,3},{3,0},{4,5},{5,6},{6,7},{7,4},{8,9},{9,10},{10,1... | collective-permute-start | bytes 3538952 | tf_op jit(solution)/shard_map/ppermute | solution.py:21
  23.0 15.6 %collective-permute-start.1 = (f32[384,768]{1,0:T(8,128)S(1)}, f32[384,768]{1,0:T(8,128)S(1)}, u32[]{:S(2)}, u32[]{:S(2)}) collective-permute-start(f32[384,768]{1,0:T(8,128)S(1)} %collective-permute-done), channel_id=1, source_target_pairs={{0,1},{1,2},{2,3},{3,0},{4,5},{5,6},{6,7},{7,4},{8,9},{9,10},{10,1... | collective-permute-start | bytes 3538952 | tf_op jit(solution)/shard_map/ppermute | solution.py:21
  38.7 15.6 %collective-permute-start.2 = (f32[384,768]{1,0:T(8,128)S(1)}, f32[384,768]{1,0:T(8,128)S(1)}, u32[]{:S(2)}, u32[]{:S(2)}) collective-permute-start(f32[384,768]{1,0:T(8,128)S(1)} %collective-permute-done.1), channel_id=1, source_target_pairs={{0,1},{1,2},{2,3},{3,0},{4,5},{5,6},{6,7},{7,4},{8,9},{9,10},{10,1... | collective-permute-start | bytes 3538952 | tf_op jit(solution)/shard_map/ppermute | solution.py:21
  72.4 0.7 copy-start.5
  72.4 387.8 %reduce-scatter.3.cloned.1.call-start = ((), (), s32[]{:S(2)}) async-start(), calls=%async_computation.3 | async-start | bytes 5898240 | tf_op jit(solution)/shard_map/reduce_scatter | solution.py:37
  246.6 28.3 %copy-start = (f32[1536,768]{1,0:T(8,128)S(1)}, f32[1536,768]{1,0:T(8,128)}, u32[]{:S(2)}) copy-start(f32[1536,768]{1,0:T(8,128)} %all-reduce.3.cloned.1.call-done) | copy-start | bytes 14155780
  246.6 55.3 %slice-start = ((s8[28311552]{0:T(1024)(128)(4,1)}), s8[4194304]{0:T(1024)(128)(4,1)S(1)}, s32[]{:S(2)}) async-start(s8[28311552]{0:T(1024)(128)(4,1)} %bitcast.56), calls=%async_computation.6 | async-start | bytes 8388608
  246.6 55.3 %slice-start.1 = ((s8[28311552]{0:T(1024)(128)(4,1)}), s8[4194304]{0:T(1024)(128)(4,1)S(1)}, s32[]{:S(2)}) async-start(s8[28311552]{0:T(1024)(128)(4,1)} %bitcast.56), calls=%async_computation.7 | async-start | bytes 8388608
  246.6 55.3 %slice-start.2 = ((s8[28311552]{0:T(1024)(128)(4,1)}), s8[4194304]{0:T(1024)(128)(4,1)S(1)}, s32[]{:S(2)}) async-start(s8[28311552]{0:T(1024)(128)(4,1)} %bitcast.56), calls=%async_computation.8 | async-start | bytes 8388608
  246.6 55.4 %slice-start.3 = ((s8[28311552]{0:T(1024)(128)(4,1)}), s8[4194304]{0:T(1024)(128)(4,1)S(1)}, s32[]{:S(2)}) async-start(s8[28311552]{0:T(1024)(128)(4,1)} %bitcast.56), calls=%async_computation.9 | async-start | bytes 8388608
  274.9 27.1 %slice-start.4 = ((s8[28311552]{0:T(1024)(128)(4,1)}), s8[4194304]{0:T(1024)(128)(4,1)S(1)}, s32[]{:S(2)}) async-start(s8[28311552]{0:T(1024)(128)(4,1)} %bitcast.56), calls=%async_computation.10 | async-start | bytes 8388608
  274.9 27.1 %slice-start.5 = ((s8[28311552]{0:T(1024)(128)(4,1)}), s8[4194304]{0:T(1024)(128)(4,1)S(1)}, s32[]{:S(2)}) async-start(s8[28311552]{0:T(1024)(128)(4,1)} %bitcast.56), calls=%async_computation.11 | async-start | bytes 8388608
  274.9 27.1 %slice-start.6 = ((s8[28311552]{0:T(1024)(128)(4,1)}), s8[3145728]{0:T(1024)(128)(4,1)S(1)}, s32[]{:S(2)}) async-start(s8[28311552]{0:T(1024)(128)(4,1)} %bitcast.56), calls=%async_computation.12 | async-start | bytes 6291456
  413.2 47.1 %copy-start.4 = (f32[384,768]{1,0:T(8,128)S(1)}, f32[384,768]{1,0:T(8,128)}, u32[]{:S(2)}) copy-start(f32[384,768]{1,0:T(8,128)} %param.4) | copy-start | bytes 3538948
  413.2 284.4 %all-reduce.5.cloned.1.call-start = ((), (), s32[]{:S(2)}) async-start(), calls=%async_computation.4 | async-start | bytes 9437184 | tf_op jit(solution)/shard_map/psum | solution.py:29
  461.7 47.0 %copy-start.2 = (f32[384,768]{1,0:T(8,128)}, f32[384,768]{1,0:T(8,128)S(1)}, u32[]{:S(2)}) copy-start(f32[384,768]{1,0:T(8,128)S(1)} %sub.25) | copy-start | bytes 3538948
  461.7 15.7 %collective-permute-start.3 = (f32[384,768]{1,0:T(8,128)S(1)}, f32[384,768]{1,0:T(8,128)S(1)}, u32[]{:S(2)}, u32[]{:S(2)}) collective-permute-start(f32[384,768]{1,0:T(8,128)S(1)} %sub.25), channel_id=1, source_target_pairs={{0,1},{1,2},{2,3},{3,0},{4,5},{5,6},{6,7},{7,4},{8,9},{9,10},{10,1... | collective-permute-start | bytes 3538952 | tf_op jit(solution)/shard_map/ppermute | solution.py:21
  477.4 15.6 %collective-permute-start.4 = (f32[384,768]{1,0:T(8,128)S(1)}, f32[384,768]{1,0:T(8,128)S(1)}, u32[]{:S(2)}, u32[]{:S(2)}) collective-permute-start(f32[384,768]{1,0:T(8,128)S(1)} %collective-permute-done.3), channel_id=1, source_target_pairs={{0,1},{1,2},{2,3},{3,0},{4,5},{5,6},{6,7},{7,4},{8,9},{9,10},{10,1... | collective-permute-start | bytes 3538952 | tf_op jit(solution)/shard_map/ppermute | solution.py:21
  493.0 15.6 %collective-permute-start.5 = (f32[384,768]{1,0:T(8,128)S(1)}, f32[384,768]{1,0:T(8,128)S(1)}, u32[]{:S(2)}, u32[]{:S(2)}) collective-permute-start(f32[384,768]{1,0:T(8,128)S(1)} %collective-permute-done.4), channel_id=1, source_target_pairs={{0,1},{1,2},{2,3},{3,0},{4,5},{5,6},{6,7},{7,4},{8,9},{9,10},{10,1... | collective-permute-start | bytes 3538952 | tf_op jit(solution)/shard_map/ppermute | solution.py:21
  525.5 386.2 %reduce-scatter.5.cloned.1.call-start = ((), (), s32[]{:S(2)}) async-start(), calls=%async_computation.5 | async-start | bytes 5898240 | tf_op jit(solution)/shard_map/reduce_scatter | solution.py:37
  697.6 28.6 %copy-start.1 = (f32[1536,768]{1,0:T(8,128)S(1)}, f32[1536,768]{1,0:T(8,128)}, u32[]{:S(2)}) copy-start(f32[1536,768]{1,0:T(8,128)} %all-reduce.5.cloned.1.call-done) | copy-start | bytes 14155780
  697.6 55.9 %slice-start.7 = ((s8[28311552]{0:T(1024)(128)(4,1)}), s8[4194304]{0:T(1024)(128)(4,1)S(1)}, s32[]{:S(2)}) async-start(s8[28311552]{0:T(1024)(128)(4,1)} %bitcast.58), calls=%async_computation.13 | async-start | bytes 8388608
  697.6 55.9 %slice-start.8 = ((s8[28311552]{0:T(1024)(128)(4,1)}), s8[4194304]{0:T(1024)(128)(4,1)S(1)}, s32[]{:S(2)}) async-start(s8[28311552]{0:T(1024)(128)(4,1)} %bitcast.58), calls=%async_computation.14 | async-start | bytes 8388608
  697.6 55.9 %slice-start.9 = ((s8[28311552]{0:T(1024)(128)(4,1)}), s8[4194304]{0:T(1024)(128)(4,1)S(1)}, s32[]{:S(2)}) async-start(s8[28311552]{0:T(1024)(128)(4,1)} %bitcast.58), calls=%async_computation.15 | async-start | bytes 8388608
  697.6 55.9 %slice-start.10 = ((s8[28311552]{0:T(1024)(128)(4,1)}), s8[4194304]{0:T(1024)(128)(4,1)S(1)}, s32[]{:S(2)}) async-start(s8[28311552]{0:T(1024)(128)(4,1)} %bitcast.58), calls=%async_computation.16 | async-start | bytes 8388608
  726.1 27.4 %slice-start.11 = ((s8[28311552]{0:T(1024)(128)(4,1)}), s8[4194304]{0:T(1024)(128)(4,1)S(1)}, s32[]{:S(2)}) async-start(s8[28311552]{0:T(1024)(128)(4,1)} %bitcast.58), calls=%async_computation.17 | async-start | bytes 8388608
  726.1 27.4 %slice-start.12 = ((s8[28311552]{0:T(1024)(128)(4,1)}), s8[4194304]{0:T(1024)(128)(4,1)S(1)}, s32[]{:S(2)}) async-start(s8[28311552]{0:T(1024)(128)(4,1)} %bitcast.58), calls=%async_computation.18 | async-start | bytes 8388608
  726.1 27.4 %slice-start.13 = ((s8[28311552]{0:T(1024)(128)(4,1)}), s8[3145728]{0:T(1024)(128)(4,1)S(1)}, s32[]{:S(2)}) async-start(s8[28311552]{0:T(1024)(128)(4,1)} %bitcast.58), calls=%async_computation.19 | async-start | bytes 6291456
  864.6 47.1 %copy-start.3 = (f32[384,768]{1,0:T(8,128)S(1)}, f32[384,768]{1,0:T(8,128)}, u32[]{:S(2)}) copy-start(f32[384,768]{1,0:T(8,128)} %copy-done.2) | copy-start | bytes 3538948
Sparse Core Ops, SparseCore 0:
  72.5 174.0 all-reduce.2
  413.3 46.8 reduce-scatter.2
  525.6 171.9 all-reduce.4
  864.7 46.9 reduce-scatter.4
